TPU v7x, 256 devices: a whole 4x4x8 slice. The times are simulated.
256 devices in a mesh: leaf: 64 (over z, x, core), level: 4 (over y).
Axes of the slice: x: 4, y: 4, z: 8, core: 2. Of those that a mesh axis runs over, the one named last changes fastest.
Arguments:
- charges: bfloat16 [3072, 128, 256], P(('leaf', 'level')), may hold values from -6 to 6
- near_mat: bfloat16 [3072, 16, 128, 128], P(('leaf', 'level')), may hold values from -0.1875 to 0.1875
- near_source: int32 [3072, 16], P(('leaf', 'level')), may hold values from 0 to 143
- near_count: int32 [3072], P(('leaf', 'level')), may hold values from 1 to 16, as said below
- moment_map: bfloat16 [3072, 256, 128], P(('leaf', 'level')), may hold values from -0.078125 to 0.078125
- local_eval: bfloat16 [3072, 128, 256], P(('leaf', 'level')), may hold values from -0.375 to 0.375
- upward_child_translation: bfloat16 [8, 256, 256], replicated, may hold values from -0.125 to 0.125
- shift_down: bfloat16 [8, 256, 256], replicated, may hold values from -0.375 to 0.375
- transfer_ops: bfloat16 [8, 256, 256], replicated, may hold values from -0.0625 to 0.0625
- subtree_interaction_list: int32 [64, 32], P('leaf'), may hold values from 0 to 63
- subtree_interaction_operators: int32 [64, 32], P('leaf'), may hold values from 0 to 7
- parent_list: int32 [64, 8], P('leaf'), may hold values from 0 to 7
- parent_ops: int32 [64, 8], P('leaf'), may hold values from 0 to 7
Outputs:
- potential: float32 [3072, 128, 256], P(('leaf', 'level'))
Inputs may be any that keep to these rules, and one draw needn't show every extreme that they name: `near_count`: some block uses all 16 slots and some block only one.
All inputs are finite; a program needn't handle non-finite values.
Results may differ from a plain program's by a relative error of at most 0.012.
Values may be sent and summed in bfloat16 or wider, within the bound.
No kernel may reach another device: no remote copies, remote signals or barrier semaphores. Data moves between devices by JAX's collectives and lax.ppermute only.
A program may use at most 128 MiB of HBM per device.

v0:
```python
import jax
import jax.numpy as jnp
from jax import lax
from jax.sharding import PartitionSpec as P


def extended_2(cells, sides, width):
    for axis, dim in sides:
        count = lax.axis_size(axis)
        ends = count - 1
        head = lax.slice_in_dim(cells, 0, width, axis=dim)
        tail = lax.slice_in_dim(cells, cells.shape[dim] - width, cells.shape[dim], axis=dim)
        cells = jnp.concatenate(
            [
                lax.ppermute(tail, axis, [(i, (i + 1) % count) for i in range(ends)]),
                cells,
                lax.ppermute(head, axis, [((i + 1) % count, i) for i in range(ends)]),
            ],
            axis=dim,
        )
    return cells


def top_tree(
    every,
    upward_child_translation,
    shift_down,
    transfer_ops,
    subtree_interaction_list,
    subtree_interaction_operators,
    parent_list,
    parent_ops,
    leaf_index,
):
    leaves, coeffs, columns = every.shape
    grouped_terms = every.reshape(leaves // 8, 8, coeffs, columns)
    upper_levels = jnp.einsum(
        "get,kgtv->kev", upward_child_translation, grouped_terms, preferred_element_type=jnp.float32
    ).astype(jnp.bfloat16)
    coarse = jnp.einsum(
        "kcd,kdr->cr",
        transfer_ops[parent_ops[0]],
        upper_levels[parent_list[0]],
        preferred_element_type=jnp.float32,
    ).astype(jnp.bfloat16)
    far_leaf = jnp.einsum(
        "kcd,kdr->cr",
        transfer_ops[subtree_interaction_operators[0]],
        every[subtree_interaction_list[0]],
        preferred_element_type=jnp.float32,
    )
    downward = jnp.dot(shift_down[leaf_index % 8], coarse, preferred_element_type=jnp.float32)
    return (far_leaf + downward).astype(jnp.bfloat16)


def on_device(
    charges,
    near_mat,
    near_source,
    near_count,
    moment_map,
    local_eval,
    upward_child_translation,
    shift_down,
    transfer_ops,
    subtree_interaction_list,
    subtree_interaction_operators,
    parent_list,
    parent_ops,
):
    slots = near_mat.shape[1]
    subtree = lax.all_gather(charges, "level", axis=0, tiled=True)
    extended = extended_2(subtree, (("leaf", 0),), subtree.shape[0])
    picked = extended[near_source]
    active = (jnp.arange(slots, dtype=jnp.int32)[None, :] < near_count[:, None]).astype(
        jnp.bfloat16
    )
    picked = picked * active[:, :, None, None]
    near_part = jnp.einsum("bkpq,bkqr->bpr", near_mat, picked, preferred_element_type=jnp.float32)
    partial_moment = jnp.einsum(
        "bcp,bpr->cr", moment_map, charges, preferred_element_type=jnp.float32
    )
    leaf_index = lax.axis_index("leaf")
    moment = lax.psum(partial_moment.astype(jnp.bfloat16), "level")
    every = lax.all_gather(moment[None], "leaf", axis=0, tiled=True)
    local_part = top_tree(
        every,
        upward_child_translation,
        shift_down,
        transfer_ops,
        subtree_interaction_list,
        subtree_interaction_operators,
        parent_list,
        parent_ops,
        leaf_index,
    )
    far_part = jnp.einsum("bpc,cr->bpr", local_eval, local_part, preferred_element_type=jnp.float32)
    return near_part + far_part


def solution(mesh):
    placed = (
        P(("leaf", "level"), None, None),
        P(("leaf", "level"), None, None, None),
        P(("leaf", "level"), None),
        P(("leaf", "level")),
        P(("leaf", "level"), None, None),
        P(("leaf", "level"), None, None),
        P(),
        P(),
        P(),
        P("leaf", None),
        P("leaf", None),
        P("leaf", None),
        P("leaf", None),
    )
    return jax.shard_map(
        on_device,
        mesh=mesh,
        in_specs=placed,
        out_specs=P(("leaf", "level"), None, None),
        check_vma=False,
    )
```

profile of v0, /device:TPU:103, one launch (start us, length us, event | category | flops | bytes accessed | tf_op | source)
XLA Modules:
  0.0 231.8 jit_solution(3247410838116859868)
XLA Ops:
  6.5 2.5 %fusion.10 = bf16[1,256,256]{2,1,0:T(8,128)(2,1)} fusion(bf16[12,256,128]{2,1,0:T(8,128)(2,1)} %param.17, bf16[12,128,256]{2,1,0:T(8,128)(2,1)} %param.13), kind=kOutput, calls=%fused_computation.20 | convolution fusion | flops 201392128 | bytes 1703936 | tf_op jit(solution)/shard_map/bcp,bpr->cr/dot_general | solution.py:80
  9.1 0.7 all-gather.3.cloned.1.call-update
  9.8 46.2 %all-reduce.2.cloned.1.call-done = bf16[1,256,256]{2,1,0:T(8,128)(2,1)} async-done(((bf16[1,256,256]{2,1,0:T(8,128)(2,1)}), bf16[1,256,256]{2,1,0:T(8,128)(2,1)}) %all-reduce.2.cloned.1.call-update) | async-done | bytes 131088 | tf_op jit(solution)/shard_map/psum | solution.py:84
  56.0 46.2 %all-gather.3.cloned.1.call-done = bf16[48,128,256]{2,1,0:T(8,128)(2,1)} async-done(((bf16[12,128,256]{2,1,0:T(8,128)(2,1)}), bf16[48,128,256]{2,1,0:T(8,128)(2,1)}) %all-gather.3.cloned.1.call-update) | async-done | bytes 3145744 | tf_op jit(solution)/shard_map/all_gather | solution.py:72
  102.2 5.1 %collective-permute-start = (bf16[48,128,256]{2,1,0:T(8,128)(2,1)}, bf16[48,128,256]{2,1,0:T(8,128)(2,1)}, u32[]{:S(2)}, u32[]{:S(2)}) collective-permute-start(bf16[48,128,256]{2,1,0:T(8,128)(2,1)} %all-gather.3.cloned.1.call-done), channel_id=1, source_target_pairs={{0,4},{4,8},{8,12},{12,16},{16,20},{20,24},{24,28},{28,32},{32,36}... | collective-permute-start | bytes 9437192 | tf_op jit(solution)/shard_map/ppermute | solution.py:15
  107.3 1.9 collective-permute-start.1
  109.3 0.7 fusion.15
  110.0 2.9 %gather_fusion.1 = bf16[32,256,256]{2,1,0:T(8,128)(2,1)} fusion(bf16[8,256,256]{2,1,0:T(8,128)(2,1)S(1)} %copy-done, s32[1024]{0:T(1024)S(1)} %pad_clamp_fusion.3), kind=kCustom, calls=%fused_computation.1 | custom fusion | bytes 8388736 | tf_op jit(solution)/shard_map/gather | solution.py:48
  112.9 0.6 gather_fusion.3
  113.6 0.1 reshape.140
  113.8 33.0 %collective-permute-done = bf16[48,128,256]{2,1,0:T(8,128)(2,1)} collective-permute-done((bf16[48,128,256]{2,1,0:T(8,128)(2,1)}, bf16[48,128,256]{2,1,0:T(8,128)(2,1)}, u32[]{:S(2)}, u32[]{:S(2)}) %collective-permute-start) | collective-permute-done | bytes 3145760 | tf_op jit(solution)/shard_map/ppermute | solution.py:15
  146.8 7.7 %collective-permute-done.1 = bf16[48,128,256]{2,1,0:T(8,128)(2,1)} collective-permute-done((bf16[48,128,256]{2,1,0:T(8,128)(2,1)}, bf16[48,128,256]{2,1,0:T(8,128)(2,1)}, u32[]{:S(2)}, u32[]{:S(2)}) %collective-permute-start.1) | collective-permute-done | bytes 3145760 | tf_op jit(solution)/shard_map/ppermute | solution.py:17
  154.5 8.4 %pad_maximum_fusion = bf16[144,128,256]{2,1,0:T(8,128)(2,1)} fusion(bf16[48,128,256]{2,1,0:T(8,128)(2,1)} %collective-permute-done.1, bf16[48,128,256]{2,1,0:T(8,128)(2,1)} %all-gather.3.cloned.1.call-done, bf16[48,128,256]{2,1,0:T(8,128)(2,1)} %collective-permute-done), kind=kLoop, calls=%fused_computation.7 | loop fusion | flops 9437184 | bytes 18874368 | tf_op jit(solution)/shard_map/concatenate | solution.py:13
  162.9 12.0 %gather_fusion = bf16[192,128,256]{2,1,0:T(8,128)(2,1)} fusion(bf16[144,128,256]{2,1,0:T(8,128)(2,1)} %pad_maximum_fusion, s32[1024]{0:T(1024)S(1)} %pad_clamp_fusion.4), kind=kCustom, calls=%fused_computation | custom fusion | bytes 25166592 | tf_op jit(solution)/shard_map/gather | solution.py:74
  174.9 16.8 %copy.16 = bf16[12,16,128,256]{2,3,1,0:T(8,128)(2,1)} copy(bf16[12,16,128,256]{3,2,1,0:T(8,128)(2,1)} %bitcast.66) | data formatting | bytes 25165824 | tf_op jit(solution)/shard_map/gather | solution.py:74
  191.6 6.1 %gather_fusion.2 = bf16[32,256,256]{2,1,0:T(8,128)(2,1)} fusion(bf16[64,256,256]{2,1,0:T(8,128)(2,1)} %all-gather.5.cloned.1.call-done, s32[1024]{0:T(1024)S(1)} %pad_clamp_fusion.2), kind=kCustom, calls=%fused_computation.2 | custom fusion | bytes 8388736 | tf_op jit(solution)/shard_map/gather | solution.py:49
  197.8 5.3 %convolution_bitcast_fusion.1 = f32[256,256]{0,1:T(8,128)S(1)} fusion(bf16[32,256,256]{2,1,0:T(8,128)(2,1)} %gather_fusion.1, bf16[32,256,256]{2,1,0:T(8,128)(2,1)} %gather_fusion.2), kind=kOutput, calls=%fused_computation.14 | convolution fusion | flops 1073741824 | bytes 8650752 | tf_op jit(solution)/shard_map/kcd,kdr->cr/dot_general | solution.py:46
  203.1 0.5 copy-done.2
  203.6 3.7 %fusion.5 = bf16[8,256,256]{1,2,0:T(8,128)(2,1)S(1)} fusion(bf16[8,8,256,256]{3,2,1,0:T(8,128)(2,1)S(1)} %bitcast.67, bf16[8,256,256]{2,1,0:T(8,128)(2,1)} %param.19), kind=kOutput, calls=%fused_computation.11 | convolution fusion | flops 2148007936 | bytes 10485760 | tf_op jit(solution)/shard_map/get,kgtv->kev/dot_general | solution.py:37
  207.3 0.6 gather_fusion.4
  207.9 1.7 fusion.9
  209.6 1.5 fusion.20
  211.2 11.1 %bitcast_add_fusion = f32[12,128,256]{1,2,0:T(8,128)} fusion(f32[256,12,128]{2,0,1:T(8,128)S(1)} %fusion.20, bf16[12,16,128,128]{3,2,1,0:T(8,128)(2,1)} %param.14, bf16[12,16,128,256]{2,3,1,0:T(8,128)(2,1)} %copy.16, bf16[12,16]{1,0:T(8,128)(2,1)S(1)} %fusion.14), kind=kOutput, calls=%fused_computation.10 | convolution fusion | flops 1617297408 | bytes 22020480 | tf_op jit(solution)/shard_map/bkpq,bkqr->bpr/dot_general | solution.py:79
  222.3 3.0 %copy.17 = f32[12,128,256]{2,1,0:T(8,128)} copy(f32[12,128,256]{1,2,0:T(8,128)} %bitcast_add_fusion) | data formatting | bytes 3145728 | tf_op jit(solution)/shard_map/add | solution.py:98
  (31 shorter events, 0.3 us)
Async XLA Ops:
  6.5 103.4 %copy-start = (bf16[8,256,256]{2,1,0:T(8,128)(2,1)S(1)}, bf16[8,256,256]{2,1,0:T(8,128)(2,1)}, u32[]{:S(2)}) copy-start(bf16[8,256,256]{2,1,0:T(8,128)(2,1)} %param.21) | copy-start | bytes 3145732
  6.5 49.5 %all-reduce.2.cloned.1.call-start = ((), (), s32[]{:S(2)}) async-start(), calls=%async_computation.1 | async-start | bytes 262144 | tf_op jit(solution)/shard_map/psum | solution.py:84
  9.1 93.2 %all-gather.3.cloned.1.call-start = ((), (), s32[]{:S(2)}) async-start(), calls=%async_computation | async-start | bytes 3932160 | tf_op jit(solution)/shard_map/all_gather | solution.py:72
  9.8 181.8 %all-gather.5.cloned.1.call-start = ((), (), s32[]{:S(2)}) async-start(), calls=%async_computation.2 | async-start | bytes 8519680 | tf_op jit(solution)/shard_map/all_gather | solution.py:85
  102.2 44.5 %collective-permute-start = (bf16[48,128,256]{2,1,0:T(8,128)(2,1)}, bf16[48,128,256]{2,1,0:T(8,128)(2,1)}, u32[]{:S(2)}, u32[]{:S(2)}) collective-permute-start(bf16[48,128,256]{2,1,0:T(8,128)(2,1)} %all-gather.3.cloned.1.call-done), channel_id=1, source_target_pairs={{0,4},{4,8},{8,12},{12,16},{16,20},{20,24},{24,28},{28,32},{32,36}... | collective-permute-start | bytes 9437192 | tf_op jit(solution)/shard_map/ppermute | solution.py:15
  107.3 47.1 %collective-permute-start.1 = (bf16[48,128,256]{2,1,0:T(8,128)(2,1)}, bf16[48,128,256]{2,1,0:T(8,128)(2,1)}, u32[]{:S(2)}, u32[]{:S(2)}) collective-permute-start(bf16[48,128,256]{2,1,0:T(8,128)(2,1)} %all-gather.3.cloned.1.call-done), channel_id=1, source_target_pairs={{4,0},{8,4},{12,8},{16,12},{20,16},{24,20},{28,24},{32,28},{36,32}... | collective-permute-start | bytes 9437192 | tf_op jit(solution)/shard_map/ppermute | solution.py:17
  110.0 2.9 %copy-start.5 = (s32[1,8]{1,0:T(1,128)S(1)}, s32[1,8]{1,0:T(1,128)}, u32[]{:S(2)}) copy-start(s32[1,8]{1,0:T(1,128)} %param.25) | copy-start | bytes 100
  110.0 3.6 %copy-start.3 = (s32[12,16]{1,0:T(8,128)S(1)}, s32[12,16]{1,0:T(8,128)}, u32[]{:S(2)}) copy-start(s32[12,16]{1,0:T(8,128)} %param.15) | copy-start | bytes 2308
  110.0 3.6 %copy-start.6 = (s32[1,32]{1,0:T(1,128)S(1)}, s32[1,32]{1,0:T(1,128)}, u32[]{:S(2)}) copy-start(s32[1,32]{1,0:T(1,128)} %param.22) | copy-start | bytes 388
  110.0 3.7 %copy-start.7 = (s32[1,8]{1,0:T(1,128)S(1)}, s32[1,8]{1,0:T(1,128)}, u32[]{:S(2)}) copy-start(s32[1,8]{1,0:T(1,128)} %param.24) | copy-start | bytes 100
  110.0 3.7 %copy-start.4 = (s32[12]{0:T(128)S(1)}, s32[12]{0:T(128)}, u32[]{:S(2)}) copy-start(s32[12]{0:T(128)} %param.16) | copy-start | bytes 148
  197.8 5.8 %copy-start.2 = (bf16[64,256,256]{2,1,0:T(8,128)(2,1)S(1)}, bf16[64,256,256]{2,1,0:T(8,128)(2,1)}, u32[]{:S(2)}) copy-start(bf16[64,256,256]{2,1,0:T(8,128)(2,1)} %all-gather.5.cloned.1.call-done) | copy-start | bytes 25165828
  211.1 14.2 %copy-start.1 = (bf16[8,256,256]{2,1,0:T(8,128)(2,1)S(1)}, bf16[8,256,256]{2,1,0:T(8,128)(2,1)}, u32[]{:S(2)}) copy-start(bf16[8,256,256]{2,1,0:T(8,128)(2,1)} %param.21) | copy-start | bytes 3145732
Sparse Core Ops, SparseCore 0:
  9.6 46.3 all-reduce.1
  57.8 44.3 all-gather.2
  105.0 81.0 all-gather.4
where the time goes:
time: 233 us; the launch traced here: 232 us
  waiting for transfers between devices  134 us (58%)
  local copies, waits for them, and re-layouts  42.6 us (18%)
  matrix products  25.9 us (11%)
  between operations  13.3 us (6%)
  other arithmetic  9.2 us (4%)
  starting transfers between devices  7.09 us (3%)
    all_gather x1, waiting for transfers between devices, on_device(): subtree = lax.all_gather(charges, 'level', axis=0, tiled=True)  46.2 us
    psum x1, waiting for transfers between devices, on_device(): moment = lax.psum(partial_moment.astype(jnp.bfloat16), 'level')  46.2 us
    ppermute x1, waiting for transfers between devices, extended_2(): lax.ppermute(tail, axis, [(i, (i + 1) % count) for i in range(ends)])  33 us
    gather x2, local copies, waits for them, and re-layouts, on_device(): picked = extended[near_source]  28.7 us
    dot_general x1, matrix products, on_device(): jnp.einsum('bkpq,bkqr->bpr', near_mat, picked, preferred_element_type=jnp...  11.1 us
    concatenate x1, other arithmetic, extended_2(): jnp.concatenate([lax.ppermute(tail, axis, [(i, (i + 1) % count) for i in...  8.42 us
    ppermute x1, waiting for transfers between devices, extended_2(): lax.ppermute(head, axis, [((i + 1) % count, i) for i in range(ends)])  7.72 us
    gather x1, local copies, waits for them, and re-layouts, top_tree(): every[subtree_interaction_list[0]]  6.13 us
  transfers between devices with their start and end apart: 5, of which 4 were waited for; matrix products, arithmetic and copies ran while one was open for 18% of the time, Pallas kernels for 0%

commit v1 on v0

--- a/solution.py
+++ b/solution.py
@@ -69,7 +69,9 @@
     parent_ops,
 ):
     slots = near_mat.shape[1]
-    subtree = lax.all_gather(charges, "level", axis=0, tiled=True)
+    subtree = jnp.concatenate(
+        lax.all_to_all(jnp.stack([charges] * lax.axis_size("level")), "level", 0, 0), axis=0
+    )
     extended = extended_2(subtree, (("leaf", 0),), subtree.shape[0])
     picked = extended[near_source]
     active = (jnp.arange(slots, dtype=jnp.int32)[None, :] < near_count[:, None]).astype(

time: 233 us -> 241 us (1.034)
  blocking collectives: 0 us -> 38 us
  waiting for transfers between devices: 134 us -> 102 us
  starting transfers between devices: 7.09 us -> 10.1 us
    all_gather x1 -> x0, waiting for transfers between devices: 46.2 us -> none  [on_device(): subtree = lax.all_gather(charges, 'level', axis=0, tiled=True)]
    all_to_all x0 -> x1, blocking collectives: none -> 38 us  [on_device(): lax.all_to_all(jnp.stack([charges] * lax.axis_size('level')), 'level', 0, 0)]
    ppermute x1, waiting for transfers between devices: 33 us -> 44.1 us  [extended_2(): lax.ppermute(tail, axis, [(i, (i + 1) % count) for i in range(ends)])]
    ppermute x1, starting transfers between devices: 5.09 us -> 8.14 us  [extended_2(): lax.ppermute(tail, axis, [(i, (i + 1) % count) for i in range(ends)])]
    ppermute x1, waiting for transfers between devices: 7.72 us -> 10.7 us  [extended_2(): lax.ppermute(head, axis, [((i + 1) % count, i) for i in range(ends)])]
  transfers between devices with their start and end apart: 5 -> 4, of which waited for: 4 -> 3; matrix products, arithmetic and copies ran while one was open for 18% -> 17% of each run, Pallas kernels for 0% -> 0%
where the time goes in v1:
time: 241 us; the launch traced here: 240 us
  waiting for transfers between devices  102 us (42%)
  local copies, waits for them, and re-layouts  44.6 us (19%)
  blocking collectives  38 us (16%)
  matrix products  24 us (10%)
  between operations  13.6 us (6%)
  starting transfers between devices  10.1 us (4%)
  other arithmetic  7.96 us (3%)
    psum x1, waiting for transfers between devices, on_device(): moment = lax.psum(partial_moment.astype(jnp.bfloat16), 'level')  46.9 us
    ppermute x1, waiting for transfers between devices, extended_2(): lax.ppermute(tail, axis, [(i, (i + 1) % count) for i in range(ends)])  44.1 us
    all_to_all x1, blocking collectives, on_device(): lax.all_to_all(jnp.stack([charges] * lax.axis_size('level')), 'level', 0, 0)  38 us
    gather x2, local copies, waits for them, and re-layouts, on_device(): picked = extended[near_source]  28.5 us
    dot_general x1, matrix products, on_device(): jnp.einsum('bkpq,bkqr->bpr', near_mat, picked, preferred_element_type=jnp...  11.1 us
    ppermute x1, waiting for transfers between devices, extended_2(): lax.ppermute(head, axis, [((i + 1) % count, i) for i in range(ends)])  10.7 us
    ppermute x1, starting transfers between devices, extended_2(): lax.ppermute(tail, axis, [(i, (i + 1) % count) for i in range(ends)])  8.14 us
    concatenate x1, other arithmetic, extended_2(): jnp.concatenate([lax.ppermute(tail, axis, [(i, (i + 1) % count) for i in...  7.84 us
  transfers between devices with their start and end apart: 4, of which 3 were waited for; matrix products, arithmetic and copies ran while one was open for 17% of the time, Pallas kernels for 0%

profile of v1, /device:TPU:103, one launch (start us, length us, event | category | flops | bytes accessed | tf_op | source)
XLA Modules:
  0.0 240.1 jit_solution(6402833683073933182)
XLA Ops:
  6.5 2.5 %fusion.10 = bf16[1,256,256]{2,1,0:T(8,128)(2,1)} fusion(bf16[12,256,128]{2,1,0:T(8,128)(2,1)} %param.17, bf16[12,128,256]{2,1,0:T(8,128)(2,1)} %param.13), kind=kOutput, calls=%fused_computation.20 | convolution fusion | flops 201392128 | bytes 1703936 | tf_op jit(solution)/shard_map/bcp,bpr->cr/dot_general | solution.py:82
  9.1 46.9 %all-reduce.2.cloned.1.call-done = bf16[1,256,256]{2,1,0:T(8,128)(2,1)} async-done(((bf16[1,256,256]{2,1,0:T(8,128)(2,1)}), bf16[1,256,256]{2,1,0:T(8,128)(2,1)}) %all-reduce.2.cloned.1.call-update) | async-done | bytes 131088 | tf_op jit(solution)/shard_map/psum | solution.py:86
  56.0 1.5 stack.2
  57.5 38.0 %all_to_all.5 = bf16[4,12,128,256]{3,2,1,0:T(8,128)(2,1)} all-to-all(bf16[4,12,128,256]{3,2,1,0:T(8,128)(2,1)S(1)} %stack.2), channel_id=1, replica_groups=mesh['leaf'=64,'level'=4] {'level'}, dimensions={0} | all-to-all | bytes 6291456 | tf_op jit(solution)/shard_map/all_to_all | solution.py:73
  95.5 8.1 %collective-permute-start = (bf16[48,128,256]{2,1,0:T(8,128)(2,1)}, bf16[48,128,256]{2,1,0:T(8,128)(2,1)}, u32[]{:S(2)}, u32[]{:S(2)}) collective-permute-start(bf16[48,128,256]{2,1,0:T(8,128)(2,1)} %bitcast), channel_id=1, source_target_pairs={{0,4},{4,8},{8,12},{12,16},{16,20},{20,24},{24,28},{28,32},{32,36}... | collective-permute-start | bytes 9437192 | tf_op jit(solution)/shard_map/ppermute | solution.py:15
  103.7 1.9 collective-permute-start.1
  105.7 2.9 %gather_fusion.1 = bf16[32,256,256]{2,1,0:T(8,128)(2,1)} fusion(bf16[8,256,256]{2,1,0:T(8,128)(2,1)S(1)} %copy-done, s32[1024]{0:T(1024)S(1)} %pad_clamp_fusion.3), kind=kCustom, calls=%fused_computation.1 | custom fusion | bytes 8388736 | tf_op jit(solution)/shard_map/gather | solution.py:48
  108.6 0.6 gather_fusion.3
  109.3 0.1 reshape.146
  109.5 44.1 %collective-permute-done = bf16[48,128,256]{2,1,0:T(8,128)(2,1)} collective-permute-done((bf16[48,128,256]{2,1,0:T(8,128)(2,1)}, bf16[48,128,256]{2,1,0:T(8,128)(2,1)}, u32[]{:S(2)}, u32[]{:S(2)}) %collective-permute-start) | collective-permute-done | bytes 3145760 | tf_op jit(solution)/shard_map/ppermute | solution.py:15
  153.6 10.7 %collective-permute-done.1 = bf16[48,128,256]{2,1,0:T(8,128)(2,1)} collective-permute-done((bf16[48,128,256]{2,1,0:T(8,128)(2,1)}, bf16[48,128,256]{2,1,0:T(8,128)(2,1)}, u32[]{:S(2)}, u32[]{:S(2)}) %collective-permute-start.1) | collective-permute-done | bytes 3145760 | tf_op jit(solution)/shard_map/ppermute | solution.py:17
  164.3 7.8 %pad_maximum_fusion = bf16[144,128,256]{2,1,0:T(8,128)(2,1)} fusion(bf16[48,128,256]{2,1,0:T(8,128)(2,1)} %collective-permute-done.1, bf16[48,128,256]{2,1,0:T(8,128)(2,1)} %bitcast, bf16[48,128,256]{2,1,0:T(8,128)(2,1)} %collective-permute-done), kind=kLoop, calls=%fused_computation.7 | loop fusion | flops 9437184 | bytes 18874368 | tf_op jit(solution)/shard_map/concatenate | solution.py:13
  172.2 11.8 %gather_fusion = bf16[192,128,256]{2,1,0:T(8,128)(2,1)} fusion(bf16[144,128,256]{2,1,0:T(8,128)(2,1)} %pad_maximum_fusion, s32[1024]{0:T(1024)S(1)} %pad_clamp_fusion.4), kind=kCustom, calls=%fused_computation | custom fusion | bytes 25166592 | tf_op jit(solution)/shard_map/gather | solution.py:76
  184.0 16.7 %copy.17 = bf16[12,16,128,256]{2,3,1,0:T(8,128)(2,1)} copy(bf16[12,16,128,256]{3,2,1,0:T(8,128)(2,1)} %bitcast.68) | data formatting | bytes 25165824 | tf_op jit(solution)/shard_map/gather | solution.py:76
  200.7 6.1 %gather_fusion.2 = bf16[32,256,256]{2,1,0:T(8,128)(2,1)} fusion(bf16[64,256,256]{2,1,0:T(8,128)(2,1)} %all-gather.2.cloned.1.call-done, s32[1024]{0:T(1024)S(1)} %pad_clamp_fusion.2), kind=kCustom, calls=%fused_computation.2 | custom fusion | bytes 8388736 | tf_op jit(solution)/shard_map/gather | solution.py:49
  206.8 4.8 %convolution_bitcast_fusion.1 = f32[256,256]{1,0:T(8,128)S(1)} fusion(bf16[32,256,256]{2,1,0:T(8,128)(2,1)} %gather_fusion.1, bf16[32,256,256]{2,1,0:T(8,128)(2,1)} %gather_fusion.2), kind=kOutput, calls=%fused_computation.14 | convolution fusion | flops 1073741824 | bytes 8650752 | tf_op jit(solution)/shard_map/kcd,kdr->cr/dot_general | solution.py:46
  211.7 1.0 copy-done.2
  212.7 0.2 copy-done.5
  212.9 2.4 fusion.5
  215.3 0.6 gather_fusion.4
  215.9 1.6 fusion.9
  217.5 1.6 fusion.20
  219.1 11.1 %bitcast_add_fusion = f32[12,128,256]{1,2,0:T(8,128)} fusion(f32[256,12,128]{2,0,1:T(8,128)S(1)} %fusion.20, bf16[12,16,128,128]{3,2,1,0:T(8,128)(2,1)} %param.14, bf16[12,16,128,256]{2,3,1,0:T(8,128)(2,1)} %copy.17, bf16[12,16]{1,0:T(8,128)(2,1)S(1)} %fusion.14), kind=kOutput, calls=%fused_computation.10 | convolution fusion | flops 1617297408 | bytes 22020480 | tf_op jit(solution)/shard_map/bkpq,bkqr->bpr/dot_general | solution.py:81
  230.2 3.0 %copy.21 = f32[12,128,256]{2,1,0:T(8,128)} copy(f32[12,128,256]{1,2,0:T(8,128)} %bitcast_add_fusion) | data formatting | bytes 3145728 | tf_op jit(solution)/shard_map/add | solution.py:100
  (34 shorter events, 0.3 us)
Async XLA Ops:
  6.5 99.1 %copy-start = (bf16[8,256,256]{2,1,0:T(8,128)(2,1)S(1)}, bf16[8,256,256]{2,1,0:T(8,128)(2,1)}, u32[]{:S(2)}) copy-start(bf16[8,256,256]{2,1,0:T(8,128)(2,1)} %param.21) | copy-start | bytes 3145732
  6.5 49.5 %all-reduce.2.cloned.1.call-start = ((), (), s32[]{:S(2)}) async-start(), calls=%async_computation.1 | async-start | bytes 262144 | tf_op jit(solution)/shard_map/psum | solution.py:86
  9.1 191.7 %all-gather.2.cloned.1.call-start = ((), (), s32[]{:S(2)}) async-start(), calls=%async_computation.2 | async-start | bytes 8519680 | tf_op jit(solution)/shard_map/all_gather | solution.py:87
  56.0 49.6 %copy-start.6 = (s32[1,32]{1,0:T(1,128)S(1)}, s32[1,32]{1,0:T(1,128)}, u32[]{:S(2)}) copy-start(s32[1,32]{1,0:T(1,128)} %param.23) | copy-start | bytes 388
  95.5 58.1 %collective-permute-start = (bf16[48,128,256]{2,1,0:T(8,128)(2,1)}, bf16[48,128,256]{2,1,0:T(8,128)(2,1)}, u32[]{:S(2)}, u32[]{:S(2)}) collective-permute-start(bf16[48,128,256]{2,1,0:T(8,128)(2,1)} %bitcast), channel_id=1, source_target_pairs={{0,4},{4,8},{8,12},{12,16},{16,20},{20,24},{24,28},{28,32},{32,36}... | collective-permute-start | bytes 9437192 | tf_op jit(solution)/shard_map/ppermute | solution.py:15
  103.7 60.7 %collective-permute-start.1 = (bf16[48,128,256]{2,1,0:T(8,128)(2,1)}, bf16[48,128,256]{2,1,0:T(8,128)(2,1)}, u32[]{:S(2)}, u32[]{:S(2)}) collective-permute-start(bf16[48,128,256]{2,1,0:T(8,128)(2,1)} %bitcast), channel_id=1, source_target_pairs={{4,0},{8,4},{12,8},{16,12},{20,16},{24,20},{28,24},{32,28},{36,32}... | collective-permute-start | bytes 9437192 | tf_op jit(solution)/shard_map/ppermute | solution.py:17
  105.7 2.9 %copy-start.7 = (s32[1,8]{1,0:T(1,128)S(1)}, s32[1,8]{1,0:T(1,128)}, u32[]{:S(2)}) copy-start(s32[1,8]{1,0:T(1,128)} %param.25) | copy-start | bytes 100
  105.7 3.6 %copy-start.3 = (s32[12,16]{1,0:T(8,128)S(1)}, s32[12,16]{1,0:T(8,128)}, u32[]{:S(2)}) copy-start(s32[12,16]{1,0:T(8,128)} %param.15) | copy-start | bytes 2308
  105.7 3.6 %copy-start.8 = (s32[1,32]{1,0:T(1,128)S(1)}, s32[1,32]{1,0:T(1,128)}, u32[]{:S(2)}) copy-start(s32[1,32]{1,0:T(1,128)} %param.22) | copy-start | bytes 388
  105.7 3.7 %copy-start.9 = (s32[1,8]{1,0:T(1,128)S(1)}, s32[1,8]{1,0:T(1,128)}, u32[]{:S(2)}) copy-start(s32[1,8]{1,0:T(1,128)} %param.24) | copy-start | bytes 100
  105.7 3.7 %copy-start.4 = (s32[12]{0:T(128)S(1)}, s32[12]{0:T(128)}, u32[]{:S(2)}) copy-start(s32[12]{0:T(128)} %param.16) | copy-start | bytes 148
  206.8 5.8 %copy-start.2 = (bf16[64,256,256]{2,1,0:T(8,128)(2,1)S(1)}, bf16[64,256,256]{2,1,0:T(8,128)(2,1)}, u32[]{:S(2)}) copy-start(bf16[64,256,256]{2,1,0:T(8,128)(2,1)} %all-gather.2.cloned.1.call-done) | copy-start | bytes 25165828
  206.8 6.1 %copy-start.5 = (bf16[8,256,256]{2,1,0:T(8,128)(2,1)S(1)}, bf16[8,256,256]{2,1,0:T(8,128)(2,1)}, u32[]{:S(2)}) copy-start(bf16[8,256,256]{2,1,0:T(8,128)(2,1)} %param.19) | copy-start | bytes 3145732
  219.1 14.2 %copy-start.1 = (bf16[8,256,256]{2,1,0:T(8,128)(2,1)S(1)}, bf16[8,256,256]{2,1,0:T(8,128)(2,1)}, u32[]{:S(2)}) copy-start(bf16[8,256,256]{2,1,0:T(8,128)(2,1)} %param.21) | copy-start | bytes 3145732
Sparse Core Ops, SparseCore 0:
  9.6 46.3 all-reduce.1
  58.8 108.4 all-gather.1
